TPU v7x, 32 devices: a whole 2x2x4 slice. The times are simulated.
32 devices in a mesh: mesh: 8 (over y, x, core), band: 4 (over z).
Axes of the slice: x: 2, y: 2, z: 4, core: 2. Of those that a mesh axis runs over, the one named last changes fastest.
Arguments:
- orbitals: bfloat16 [8, 512, 2048], P('mesh', None, 'band'), may hold values from -6 to 6
- element_matrix: bfloat16 [8, 512, 512], P('mesh'), may hold values from -0.25 to 0.25
- face_map: int32 [8, 64], P('mesh'), may hold values from 0 to 63, as said below
- panel_order: int32 [4], replicated, may hold values from 0 to 15, as said below
Outputs:
- filtered: bfloat16 [8, 512, 2048], P('mesh', None, 'band')
- margin: float32 [2048, 512], P('band')
Inputs may be any that keep to these rules, and one draw needn't show every extreme that they name: `face_map`: each row is a permutation of 0 to 63. `panel_order`: the entries are distinct; the last panel, 2048 // 128 - 1, is always among them.
All inputs are finite; a program needn't handle non-finite values.
Results may differ from a plain program's by a relative error of at most 0.0045.
Values may be sent and summed in bfloat16 or wider, within the bound.
A program may use at most 64 MiB of HBM per device.

v0:
```python
import jax
import jax.numpy as jnp
from jax import lax
from jax.sharding import PartitionSpec as P

PANEL = 128
PANELS = 4


center_value = 0.5
half_width = 2.0


def passed_along(shard, axis, by):
    devices = lax.axis_size(axis)
    return lax.ppermute(shard, axis, [(i, (i + by) % devices) for i in range(devices)])


def from_root(value, axis, source):
    kept = jnp.where(lax.axis_index(axis) == source, value, 0).astype(value.dtype)
    return lax.psum(kept, axis)


def operate(matrices, one_hot, values):
    partial_value = jnp.einsum("enm,emo->eno", matrices, values, preferred_element_type=jnp.float32)
    elem_count, node_count, orb_count = partial_value.shape
    face_count = one_hot.shape[1]
    partial_value = partial_value.reshape(
        elem_count, node_count // face_count, face_count, orb_count
    )
    top_face = partial_value[:, -1]
    low_face = partial_value[:, 0]
    moved_top = jnp.einsum("gfj,gfo->gjo", one_hot, top_face, precision=lax.Precision.HIGHEST)
    from_above = passed_along(low_face[0], "mesh", -1)
    upper_next = jnp.concatenate([low_face[1:], from_above[None]], 0)
    summed = top_face + jnp.einsum(
        "gfj,gjo->gfo", one_hot, upper_next, precision=lax.Precision.HIGHEST
    )
    from_below = passed_along(moved_top[-1].astype(jnp.bfloat16), "mesh", 1).astype(jnp.float32)
    lower_new = low_face + jnp.concatenate([from_below[None], moved_top[:-1]], 0)
    partial_value = partial_value.at[:, 0].set(lower_new).at[:, -1].set(summed)
    return partial_value.reshape(elem_count, node_count, orb_count)


def mesh_block_total(block):
    return lax.psum(block, "mesh")


def on_device(orbitals, element_matrix, face_map, panel_order):
    face_count = face_map.shape[1]
    one_hot = (
        face_map[:, :, None] == jnp.arange(face_count, dtype=jnp.int32)[None, None, :]
    ).astype(jnp.float32)
    start = orbitals.astype(jnp.float32)
    first = (
        (operate(element_matrix, one_hot, orbitals) - center_value * start) / half_width
    ).astype(jnp.bfloat16)
    first_wide = first.astype(jnp.float32)
    second = (
        2.0 * (operate(element_matrix, one_hot, first) - center_value * first_wide) / half_width
        - start
    )
    filtered = second.astype(jnp.bfloat16)
    elem_count, node_count, orb_count = filtered.shape
    flat = filtered.reshape(elem_count * node_count, orb_count)
    per_owner = orb_count // PANEL
    blocks = []
    for panel_step in range(PANELS):
        chosen = panel_order[panel_step]
        owner = chosen // per_owner
        offset = chosen % per_owner * PANEL
        piece = lax.dynamic_slice_in_dim(flat, offset, PANEL, 1)
        arrived = from_root(piece, "band", owner)
        product = lax.dot_general(
            flat, arrived, (((0,), (0,)), ((), ())), preferred_element_type=jnp.float32
        )
        product = mesh_block_total(product)
        blocks.append(product)
    margin = jnp.concatenate(blocks, 1)
    scale = float(elem_count * node_count * lax.axis_size("mesh")) ** (-0.5)
    return (filtered, margin * scale)


def solution(mesh):
    in_specs = (P("mesh", None, "band"), P("mesh", None, None), P("mesh", None), P())
    out_specs = (P("mesh", None, "band"), P("band", None))
    return jax.shard_map(
        on_device, mesh=mesh, in_specs=in_specs, out_specs=out_specs, check_vma=False
    )
```

profile of v0, /device:TPU:0, one launch (start us, length us, event | category | flops | bytes accessed | tf_op | source)
XLA Modules:
  0.0 146.9 jit_solution(18149578145548745626)
XLA Ops:
  7.2 0.0 copy-start
  7.2 0.0 all-reduce.7.cloned.1.call-start
  7.2 1.0 copy-done
  8.2 1.5 %convolution_bitcast_fusion = f32[1,8,64,512]{3,2,1,0:T(8,128)S(1)} fusion(bf16[8,64,512]{2,1,0:T(8,128)(2,1)S(1)} %bitcast.81, bf16[1,512,512]{2,1,0:T(8,128)(2,1)} %param.12), kind=kOutput, calls=%fused_computation | convolution fusion | flops 268435456 | bytes 2097152 | tf_op jit(solution)/shard_map/enm,emo->eno/dot_general | solution.py:25
  9.7 0.0 copy-start.6
  9.7 0.6 copy-done.6
  10.3 0.3 convolution_convert_fusion.1
  10.7 0.5 collective-permute-start
  11.2 2.9 %collective-permute-start.1 = (f32[64,512]{1,0:T(8,128)S(1)}, f32[64,512]{1,0:T(8,128)S(1)}, u32[]{:S(2)}, u32[]{:S(2)}) collective-permute-start(f32[64,512]{1,0:T(8,128)S(1)} %slice_bitcast_fusion.3), channel_id=1, source_target_pairs={{0,28},{4,0},{8,4},{12,8},{16,12},{20,16},{24,20},{28,24},{1,29},{... | collective-permute-start | bytes 393224 | tf_op jit(solution)/shard_map/ppermute | solution.py:16
  14.2 0.0 copy-start.7
  14.2 0.1 copy.6
  14.2 0.6 copy-done.7
  14.8 0.0 copy-start.2
  14.8 0.7 fusion.27
  26.3 0.0 collective-permute-done
  26.3 0.0 collective-permute-done.1
  26.3 0.2 fusion.3
  26.6 0.0 copy-done.2
  26.6 0.2 fusion.6
  26.8 0.4 fusion.16
  27.2 0.3 convolution_convert_fusion
  27.6 0.1 collective-permute-start.2
  27.6 0.1 copy.8
  27.8 2.7 %collective-permute-start.3 = (f32[64,512]{1,0:T(8,128)S(1)}, f32[64,512]{1,0:T(8,128)S(1)}, u32[]{:S(2)}, u32[]{:S(2)}) collective-permute-start(f32[64,512]{1,0:T(8,128)S(1)} %slice_bitcast_fusion.1), channel_id=1, source_target_pairs={{0,28},{4,0},{8,4},{12,8},{16,12},{20,16},{24,20},{28,24},{1,29},{... | collective-permute-start | bytes 393224 | tf_op jit(solution)/shard_map/ppermute | solution.py:16
  30.4 1.8 %collective-permute-done.2 = bf16[64,512]{1,0:T(8,128)(2,1)S(1)} collective-permute-done((bf16[64,512]{1,0:T(8,128)(2,1)S(1)}, bf16[64,512]{1,0:T(8,128)(2,1)S(1)}, u32[]{:S(2)}, u32[]{:S(2)}) %collective-permute-start.2) | collective-permute-done | bytes 65568 | tf_op jit(solution)/shard_map/ppermute | solution.py:16
  32.2 0.7 collective-permute-done.3
  33.0 0.2 fusion.1
  33.2 0.2 fusion.7
  33.5 0.0 copy-start.1
  33.5 0.9 select_bitcast_fusion.3
  34.4 0.0 all-reduce.7.cloned.1.call-update
  34.4 0.0 all-reduce.5.cloned.1.call-start
  34.5 41.3 %all-reduce.7.cloned.1.call-done = (bf16[512,128]{1,0:T(8,128)(2,1)}, bf16[512,128]{1,0:T(8,128)(2,1)}, bf16[512,128]{1,0:T(8,128)(2,1)}, bf16[512,128]{1,0:T(8,128)(2,1)}) async-done(((bf16[512,128]{1,0:T(8,128)(2,1)}, bf16[512,128]{1,0:T(8,128)(2,1)}, bf16[512,128]{1,0:T(8,128)(2,1)}, bf16[512,128]{1,0:T(8,128)(2,1)}), (bf16[512,128]{1,0:T(8,128)(2,1)}, bf16[512,128]{1,0:T(8,128)(2,1)}, ...) | async-done | bytes 524304 | tf_op jit(solution)/shard_map/psum | solution.py:21
  75.7 0.0 copy-start.5
  75.7 2.0 %fusion.14 = f32[512,128]{1,0:T(8,128)} fusion(bf16[512,128]{1,0:T(8,128)(2,1)} %get-tuple-element.57, bf16[1,512,512]{2,1,0:T(8,128)(2,1)S(1)} %fusion.7), kind=kOutput, calls=%fused_computation.23 | convolution fusion | flops 67108864 | bytes 917504 | tf_op jit(solution)/shard_map/dot_general | solution.py:74
  77.7 0.0 copy-done.5
  77.7 0.0 copy-start.4
  77.7 1.0 fusion.12
  78.8 0.0 copy-done.4
  78.8 0.0 copy-start.3
  78.8 1.0 fusion.10
  79.8 0.0 copy-done.1
  79.8 0.0 copy-done.3
  79.8 1.0 fusion.8
  80.9 0.0 all-reduce.5.cloned.1.call-update
  80.9 56.9 %all-reduce.5.cloned.1.call-done = (f32[512,128]{1,0:T(8,128)}, f32[512,128]{1,0:T(8,128)}, f32[512,128]{1,0:T(8,128)}, f32[512,128]{1,0:T(8,128)}) async-done(((f32[512,128]{1,0:T(8,128)}, f32[512,128]{1,0:T(8,128)}, f32[512,128]{1,0:T(8,128)}, f32[512,128]{1,0:T(8,128)}), (f32[512,128]{1,0:T(8,128)}, f32[512,128]{1,0:T(8,128)}, f32[512,128]{1,0:T(8,128)}, ...) | async-done | bytes 1048592 | tf_op jit(solution)/shard_map/psum | solution.py:46
  137.8 2.2 %maximum_multiply_fusion = f32[512,512]{1,0:T(8,128)} fusion(f32[512,128]{1,0:T(8,128)} %get-tuple-element.50, f32[512,128]{1,0:T(8,128)} %get-tuple-element.51, f32[512,128]{1,0:T(8,128)} %get-tuple-element.52, f32[512,128]{1,0:T(8,128)} %get-tuple-element.53), kind=kLoop, calls=%fused_computation.15 | loop fusion | flops 1048576 | bytes 2097152 | tf_op jit(solution)/shard_map/mul | solution.py:81
  (4 shorter events, 0.0 us)
Async XLA Ops:
  7.2 1.0 copy-start
  7.2 68.6 %all-reduce.7.cloned.1.call-start = ((), (), s32[]{:S(2)}) async-start(), calls=%async_computation.1 | async-start | bytes 1048576 | tf_op jit(solution)/shard_map/psum | solution.py:21
  9.7 0.7 copy-start.6
  10.7 15.6 %collective-permute-start = (bf16[64,512]{1,0:T(8,128)(2,1)S(1)}, bf16[64,512]{1,0:T(8,128)(2,1)S(1)}, u32[]{:S(2)}, u32[]{:S(2)}) collective-permute-start(bf16[64,512]{1,0:T(8,128)(2,1)S(1)} %convolution_convert_fusion.1), channel_id=1, source_target_pairs={{0,4},{4,8},{8,12},{12,16},{16,20},{20,24},{24,28},{28,0},{1,5},{5... | collective-permute-start | bytes 196616 | tf_op jit(solution)/shard_map/ppermute | solution.py:16
  11.2 15.1 %collective-permute-start.1 = (f32[64,512]{1,0:T(8,128)S(1)}, f32[64,512]{1,0:T(8,128)S(1)}, u32[]{:S(2)}, u32[]{:S(2)}) collective-permute-start(f32[64,512]{1,0:T(8,128)S(1)} %slice_bitcast_fusion.3), channel_id=1, source_target_pairs={{0,28},{4,0},{8,4},{12,8},{16,12},{20,16},{24,20},{28,24},{1,29},{... | collective-permute-start | bytes 393224 | tf_op jit(solution)/shard_map/ppermute | solution.py:16
  14.2 0.7 copy-start.7
  14.8 11.8 %copy-start.2 = (bf16[1,512,512]{2,1,0:T(8,128)(2,1)S(1)}, bf16[1,512,512]{2,1,0:T(8,128)(2,1)}, u32[]{:S(2)}) copy-start(bf16[1,512,512]{2,1,0:T(8,128)(2,1)} %param.12) | copy-start | bytes 1572868
  27.6 4.6 %collective-permute-start.2 = (bf16[64,512]{1,0:T(8,128)(2,1)S(1)}, bf16[64,512]{1,0:T(8,128)(2,1)S(1)}, u32[]{:S(2)}, u32[]{:S(2)}) collective-permute-start(bf16[64,512]{1,0:T(8,128)(2,1)S(1)} %convolution_convert_fusion), channel_id=1, source_target_pairs={{0,4},{4,8},{8,12},{12,16},{16,20},{20,24},{24,28},{28,0},{1,5},{5... | collective-permute-start | bytes 196616 | tf_op jit(solution)/shard_map/ppermute | solution.py:16
  27.8 5.2 %collective-permute-start.3 = (f32[64,512]{1,0:T(8,128)S(1)}, f32[64,512]{1,0:T(8,128)S(1)}, u32[]{:S(2)}, u32[]{:S(2)}) collective-permute-start(f32[64,512]{1,0:T(8,128)S(1)} %slice_bitcast_fusion.1), channel_id=1, source_target_pairs={{0,28},{4,0},{8,4},{12,8},{16,12},{20,16},{24,20},{28,24},{1,29},{... | collective-permute-start | bytes 393224 | tf_op jit(solution)/shard_map/ppermute | solution.py:16
  33.5 46.4 %copy-start.1 = (bf16[1,512,512]{2,1,0:T(8,128)(2,1)}, bf16[1,512,512]{2,1,0:T(8,128)(2,1)S(1)}, u32[]{:S(2)}) copy-start(bf16[1,512,512]{2,1,0:T(8,128)(2,1)S(1)} %fusion.7) | copy-start | bytes 1572868
  34.4 103.4 %all-reduce.5.cloned.1.call-start = ((), (), s32[]{:S(2)}) async-start(), calls=%async_computation | async-start | bytes 2097152 | tf_op jit(solution)/shard_map/psum | solution.py:46
  75.7 2.0 %copy-start.5 = (bf16[512,128]{1,0:T(8,128)(2,1)S(1)}, bf16[512,128]{1,0:T(8,128)(2,1)}, u32[]{:S(2)}) copy-start(bf16[512,128]{1,0:T(8,128)(2,1)} %get-tuple-element.56) | copy-start | bytes 393220
  77.7 1.0 copy-start.4
  78.8 1.1 copy-start.3
Sparse Core Ops, SparseCore 0:
  34.6 41.1 all-reduce.6
  81.0 56.7 all-reduce.4
where the time goes:
time: 147 us
  waiting for transfers between devices  101 us (69%)
  between operations  25 us (17%)
  matrix products  8.15 us (6%)
  starting transfers between devices  6.3 us (4%)
  other arithmetic  3.62 us (2%)
  local copies, waits for them, and re-layouts  3.11 us (2%)
    psum x1, waiting for transfers between devices, mesh_block_total(): return lax.psum(block, 'mesh')  56.9 us
    psum x1, waiting for transfers between devices, from_root(): return lax.psum(kept, axis)  41.3 us
    ppermute x4, starting transfers between devices, passed_along(): lax.ppermute(shard, axis, [(i, (i + by) % devices) for i in range(devices)])  6.22 us
    dot_general x4, matrix products, on_device(): lax.dot_general(flat, arrived, (((0,), (0,)), ((), ())), preferred_elemen...  5.11 us
  transfers between devices with their start and end apart: 6, of which 4 were waited for; matrix products, arithmetic and copies ran while one was open for 1% of the time, Pallas kernels for 0%

commit v1 on v0

v1 whole, which is shorter than its diff:
```python
import functools

import jax
import jax.numpy as jnp
from jax import lax
from jax.experimental import pallas as pl
from jax.experimental.pallas import tpu as pltpu
from jax.sharding import PartitionSpec as P

PANEL = 128
PANELS = 4
PARTS = 4
LAG = 3
SUBLANES = 16

center_value = 0.5
half_width = 2.0

MESH = pl.DeviceIdType.MESH


def passed_along(shard, axis, by):
    devices = lax.axis_size(axis)
    return lax.ppermute(shard, axis, [(i, (i + by) % devices) for i in range(devices)])


def operate(matrices, one_hot, values):
    partial_value = jnp.einsum("enm,emo->eno", matrices, values, preferred_element_type=jnp.float32)
    elem_count, node_count, orb_count = partial_value.shape
    face_count = one_hot.shape[1]
    partial_value = partial_value.reshape(
        elem_count, node_count // face_count, face_count, orb_count
    )
    top_face = partial_value[:, -1]
    low_face = partial_value[:, 0]
    moved_top = jnp.einsum("gfj,gfo->gjo", one_hot, top_face, precision=lax.Precision.HIGHEST)
    from_above = passed_along(low_face[0], "mesh", -1)
    upper_next = jnp.concatenate([low_face[1:], from_above[None]], 0)
    summed = top_face + jnp.einsum(
        "gfj,gjo->gfo", one_hot, upper_next, precision=lax.Precision.HIGHEST
    )
    from_below = passed_along(moved_top[-1].astype(jnp.bfloat16), "mesh", 1).astype(jnp.float32)
    lower_new = low_face + jnp.concatenate([from_below[None], moved_top[:-1]], 0)
    partial_value = partial_value.at[:, 0].set(lower_new).at[:, -1].set(summed)
    return partial_value.reshape(elem_count, node_count, orb_count)


def margin_kernel(
    n, nb, groups, scale, columns_ref, f_ref, out_ref,
    own, going_up, going_down, turned, part, arrived, gathered,
    up_send, up_recv, down_send, down_recv, rs_send, rs_recv, ag_send, ag_recv,
):
    me = lax.axis_index("mesh")
    z = lax.axis_index("band")
    rows, cols = f_ref.shape
    chunk = rows // PARTS
    total = PANELS * PARTS
    slice_rows = arrived.shape[2]
    per_group = PANELS // groups
    per_panel = n // per_group

    barrier = pltpu.get_barrier_semaphore()

    @pl.loop(1, n)
    def _(d):
        pl.semaphore_signal(
            barrier, inc=1, device_id={"mesh": lax.rem(me + d, n)}, device_id_type=MESH
        )

    @pl.when(z > 0)
    def _():
        pl.semaphore_signal(barrier, inc=1, device_id={"band": z - 1}, device_id_type=MESH)

    @pl.when(z < nb - 1)
    def _():
        pl.semaphore_signal(barrier, inc=1, device_id={"band": z + 1}, device_id_type=MESH)

    here = lax.broadcasted_iota(jnp.int32, (cols, PANELS * PANEL), 0) + z * cols
    picked = jnp.dot(
        f_ref[...],
        (here == columns_ref[...]).astype(jnp.float32).astype(jnp.bfloat16),
        preferred_element_type=jnp.float32,
    ).astype(jnp.bfloat16)
    for k in range(PANELS):
        own[k * PARTS:(k + 1) * PARTS] = picked[:, k * PANEL:(k + 1) * PANEL].reshape(
            PARTS, chunk, PANEL
        )

    @pl.when(z == 0)
    def _():
        going_up[...] = own[...]

    @pl.when(z == nb - 1)
    def _():
        going_down[...] = own[...]

    pl.semaphore_wait(barrier, n - 1 + jnp.minimum(z, 1) + jnp.minimum(nb - 1 - z, 1))

    def sweep_copy(buffer, idx, send, recv, target):
        return pltpu.make_async_remote_copy(
            src_ref=buffer.at[idx], dst_ref=buffer.at[idx],
            send_sem=send.at[idx], recv_sem=recv.at[idx],
            device_id={"band": target}, device_id_type=MESH,
        )

    def pass_on(idx, buffer, send, recv, first, last, target):
        @pl.when(jnp.logical_and(idx >= 0, idx < total))
        def _():
            @pl.when(jnp.logical_not(first))
            def _():
                sweep_copy(buffer, idx, send, recv, target).wait_recv()
                buffer[idx] = own[idx] + buffer[idx]

            @pl.when(jnp.logical_not(last))
            def _():
                sweep_copy(buffer, idx, send, recv, target).start()

    above = lax.rem(z + 1, nb)
    below = lax.rem(z + nb - 1, nb)

    def step(s):
        pass_on(s - LAG * z, going_up, up_send, up_recv, z == 0, z == nb - 1, above)
        pass_on(
            s - LAG * (nb - 1 - z), going_down, down_send, down_recv, z == nb - 1, z == 0, below
        )

    def scatter_copy(g, d):
        target = lax.rem(me + d, n)
        return pltpu.make_async_remote_copy(
            src_ref=part.at[g, target], dst_ref=arrived.at[g, d],
            send_sem=rs_send.at[g, d], recv_sem=rs_recv.at[g, d],
            device_id={"mesh": target}, device_id_type=MESH,
        )

    def gather_copy(g, d, block):
        return pltpu.make_async_remote_copy(
            src_ref=gathered.at[g, block], dst_ref=gathered.at[g, block],
            send_sem=ag_send.at[g, d], recv_sem=ag_recv.at[g, d],
            device_id={"mesh": lax.rem(me + d, n)}, device_id_type=MESH,
        )

    def scatter(g):
        @pl.loop(1, n)
        def _(d):
            scatter_copy(g, d).start()

    def reduce(g):
        @pl.loop(1, n)
        def _(d):
            scatter_copy(g, d).wait_recv()
        summed = part[g, me].astype(jnp.float32)
        if n <= SUBLANES:
            for d in range(1, n):
                summed += arrived[g, d].astype(jnp.float32)
        else:
            summed = lax.fori_loop(
                1, n, lambda d, value: value + arrived[g, d].astype(jnp.float32), summed
            )
        gathered[g, me] = (summed * scale).astype(jnp.bfloat16)

        @pl.loop(1, n)
        def _(d):
            gather_copy(g, d, me).start()

    def finish(g):
        @pl.loop(1, n)
        def _(d):
            gather_copy(g, d, lax.rem(me + n - d, n)).wait_recv()
        for p in range(per_group):
            k = g * per_group + p
            block = gathered[g, p * per_panel:(p + 1) * per_panel]
            out_ref[:, k * PANEL:(k + 1) * PANEL] = block.reshape(cols, PANEL).astype(jnp.float32)

    @pl.loop(0, LAG * (nb - 1))
    def _(s):
        step(s)

    turned[...] = f_ref[...].T
    for k in range(PANELS):
        @pl.loop(LAG * (nb - 1) + k * PARTS, LAG * (nb - 1) + (k + 1) * PARTS)
        def _(s):
            step(s)
        mine = slice(k * PARTS, (k + 1) * PARTS)
        panel = (going_up[mine] + (going_down[mine] - own[mine])).reshape(rows, PANEL)
        product = jnp.dot(turned[...], panel, preferred_element_type=jnp.float32)
        g, p = k // per_group, k % per_group
        part[g, p * per_panel:(p + 1) * per_panel] = product.astype(jnp.bfloat16).reshape(
            per_panel, slice_rows, PANEL
        )
        if p == per_group - 1:
            scatter(g)
            if g > 0:
                reduce(g - 1)
            if g > 1:
                finish(g - 2)
    reduce(groups - 1)
    if groups > 1:
        finish(groups - 2)
    finish(groups - 1)

    @pl.loop(0, total)
    def _(idx):
        @pl.when(z < nb - 1)
        def _():
            sweep_copy(going_up, idx, up_send, up_recv, above).wait_send()

        @pl.when(z > 0)
        def _():
            sweep_copy(going_down, idx, down_send, down_recv, below).wait_send()

    for g in range(groups):
        @pl.loop(1, n)
        def _(d):
            scatter_copy(g, d).wait_send()
            gather_copy(g, d, me).wait_send()


def margin_of(flat, panel_order, n, nb):
    rows, cols = flat.shape
    groups = max(1, min(PANELS, PANELS * cols // (n * SUBLANES)))
    slice_rows = PANELS * cols // (groups * n)
    total = PANELS * PARTS
    scale = float(rows * n) ** (-0.5)
    sweep = pltpu.VMEM((total, rows // PARTS, PANEL), jnp.bfloat16)
    blocks = pltpu.VMEM((groups, n, slice_rows, PANEL), jnp.bfloat16)
    columns = (
        panel_order[:, None] * PANEL + jnp.arange(PANEL, dtype=jnp.int32)[None, :]
    ).reshape(1, PANELS * PANEL)
    dma = pltpu.SemaphoreType.DMA
    return pl.pallas_call(
        functools.partial(margin_kernel, n, nb, groups, scale),
        out_shape=jax.ShapeDtypeStruct((cols, PANELS * PANEL), jnp.float32),
        in_specs=[
            pl.BlockSpec(memory_space=pltpu.VMEM),
            pl.BlockSpec(memory_space=pltpu.VMEM),
        ],
        out_specs=pl.BlockSpec(memory_space=pltpu.VMEM),
        scratch_shapes=[
            sweep, sweep, sweep, pltpu.VMEM((cols, rows), jnp.bfloat16), blocks, blocks, blocks,
            dma((total,)), dma((total,)), dma((total,)), dma((total,)),
            dma((groups, n)), dma((groups, n)), dma((groups, n)), dma((groups, n)),
        ],
        compiler_params=pltpu.CompilerParams(collective_id=0, has_side_effects=True),
    )(columns, flat)


def on_device(n, nb, orbitals, element_matrix, face_map, panel_order):
    face_count = face_map.shape[1]
    one_hot = (
        face_map[:, :, None] == jnp.arange(face_count, dtype=jnp.int32)[None, None, :]
    ).astype(jnp.float32)
    start = orbitals.astype(jnp.float32)
    first = (
        (operate(element_matrix, one_hot, orbitals) - center_value * start) / half_width
    ).astype(jnp.bfloat16)
    first_wide = first.astype(jnp.float32)
    second = (
        2.0 * (operate(element_matrix, one_hot, first) - center_value * first_wide) / half_width
        - start
    )
    filtered = second.astype(jnp.bfloat16)
    elem_count, node_count, orb_count = filtered.shape
    flat = filtered.reshape(elem_count * node_count, orb_count)
    return (filtered, margin_of(flat, panel_order, n, nb))


def solution(mesh):
    in_specs = (P("mesh", None, "band"), P("mesh", None, None), P("mesh", None), P())
    out_specs = (P("mesh", None, "band"), P("band", None))
    return jax.shard_map(
        functools.partial(on_device, mesh.shape["mesh"], mesh.shape["band"]),
        mesh=mesh, in_specs=in_specs, out_specs=out_specs, check_vma=False,
    )
```

time: 147 us -> 60.9 us (0.41)
  waiting for transfers between devices: 101 us -> 4.23 us
  Pallas kernels: 0 us -> 40.1 us
  between operations: 25 us -> 0.75 us
  matrix products: 8.15 us -> 3.04 us
  other arithmetic: 3.62 us -> 1.89 us
    psum x2 -> x0, waiting for transfers between devices: 98.2 us -> none  [the longest x1 56.9 us: mesh_block_total(): return lax.psum(block, 'mesh')]
    pallas_call x0 -> x1, Pallas kernels: none -> 40.1 us  [margin_of(): pl.pallas_call(functools.partial(margin_kernel, n, nb, groups, scale), ou...]
    dot_general x4 -> x0, matrix products: 5.11 us -> none  [on_device(): lax.dot_general(flat, arrived, (((0,), (0,)), ((), ())), preferred_elemen...]
    mul x1, other arithmetic: 2.23 us -> 0.01 us  [margin_of(): panel_order[:, None] * PANEL + jnp.arange(PANEL, dtype=jnp.int32)[None, :]]
    unnamed x18 -> x11, local copies, waits for them, and re-layouts: 2.42 us -> 4.17 us
    ppermute x4, waiting for transfers between devices: 2.51 us -> 4.23 us  [passed_along(): lax.ppermute(shard, axis, [(i, (i + by) % devices) for i in range(devices)])]
  transfers between devices with their start and end apart: 6 -> 4, of which waited for: 4 -> 4; matrix products, arithmetic and copies ran while one was open for 1% -> 1% of each run, Pallas kernels for 0% -> 0%
where the time goes in v1:
time: 60.9 us; the launch traced here: 60.6 us
  Pallas kernels  40.1 us (66%)
  starting transfers between devices  6.38 us (10%)
  waiting for transfers between devices  4.23 us (7%)
  local copies, waits for them, and re-layouts  4.19 us (7%)
  matrix products  3.04 us (5%)
  other arithmetic  1.89 us (3%)
  between operations  0.75 us (1%)
    pallas_call x1, Pallas kernels, margin_of(): pl.pallas_call(functools.partial(margin_kernel, n, nb, groups, scale), ou...  40.1 us
    ppermute x4, starting transfers between devices, passed_along(): lax.ppermute(shard, axis, [(i, (i + by) % devices) for i in range(devices)])  6.38 us
    ppermute x4, waiting for transfers between devices, passed_along(): lax.ppermute(shard, axis, [(i, (i + by) % devices) for i in range(devices)])  4.23 us
    unnamed x11, local copies, waits for them, and re-layouts  4.17 us
    dot_general x2, matrix products, operate(): jnp.einsum('enm,emo->eno', matrices, values, preferred_element_type=jnp.f...  1.91 us
  transfers between devices with their start and end apart: 4, of which 4 were waited for; matrix products, arithmetic and copies ran while one was open for 1% of the time, Pallas kernels for 0%

profile of v1, /device:TPU:0, one launch (start us, length us, event | category | flops | bytes accessed | tf_op | source)
XLA Modules:
  0.0 60.6 jit_solution(11967129558929344872)
XLA Ops:
  0.6 0.0 copy-start
  0.6 1.0 %copy-done = bf16[1,512,512]{2,1,0:T(8,128)(2,1)S(1)} copy-done((bf16[1,512,512]{2,1,0:T(8,128)(2,1)S(1)}, bf16[1,512,512]{2,1,0:T(8,128)(2,1)}, u32[]{:S(2)}) %copy-start) | copy-done | bytes 524312
  1.7 1.5 %convolution_bitcast_fusion = f32[1,8,64,512]{3,2,1,0:T(8,128)S(1)} fusion(bf16[8,64,512]{2,1,0:T(8,128)(2,1)S(1)} %bitcast.58, bf16[1,512,512]{2,1,0:T(8,128)(2,1)} %param.12), kind=kOutput, calls=%fused_computation | convolution fusion | flops 268435456 | bytes 2097152 | tf_op jit(solution)/shard_map/enm,emo->eno/dot_general | solution.py:28
  3.2 0.0 copy-start.2
  3.2 0.6 %copy-done.2 = s32[1,64]{1,0:T(1,128)S(1)} copy-done((s32[1,64]{1,0:T(1,128)S(1)}, s32[1,64]{1,0:T(1,128)}, u32[]{:S(2)}) %copy-start.2) | copy-done | bytes 280
  3.8 0.3 convolution_convert_fusion.1
  4.1 0.0 copy-start.3
  4.1 0.5 collective-permute-start
  4.7 2.9 %collective-permute-start.1 = (f32[64,512]{1,0:T(8,128)S(1)}, f32[64,512]{1,0:T(8,128)S(1)}, u32[]{:S(2)}, u32[]{:S(2)}) collective-permute-start(f32[64,512]{1,0:T(8,128)S(1)} %slice_bitcast_fusion.3), channel_id=1, source_target_pairs={{0,28},{4,0},{8,4},{12,8},{16,12},{20,16},{24,20},{28,24},{1,29},{... | collective-permute-start | bytes 393224 | tf_op jit(solution)/shard_map/ppermute | solution.py:24
  7.6 0.0 copy-done.3
  7.7 0.7 %iota_add_fusion = s32[4,128]{1,0:T(4,128)} fusion(s32[4]{0:T(128)S(1)} %broadcast_multiply_fusion), kind=kLoop, calls=%fused_computation.33 | loop fusion | flops 512 | bytes 2064 | tf_op jit(solution)/shard_map/add | solution.py:227
  8.3 0.1 copy.6
  8.4 0.0 copy-start.1
  8.4 1.1 %collective-permute-done = bf16[64,512]{1,0:T(8,128)(2,1)S(1)} collective-permute-done((bf16[64,512]{1,0:T(8,128)(2,1)S(1)}, bf16[64,512]{1,0:T(8,128)(2,1)S(1)}, u32[]{:S(2)}, u32[]{:S(2)}) %collective-permute-start) | collective-permute-done | bytes 65568 | tf_op jit(solution)/shard_map/ppermute | solution.py:24
  9.5 0.6 %collective-permute-done.1 = f32[64,512]{1,0:T(8,128)S(1)} collective-permute-done((f32[64,512]{1,0:T(8,128)S(1)}, f32[64,512]{1,0:T(8,128)S(1)}, u32[]{:S(2)}, u32[]{:S(2)}) %collective-permute-start.1) | collective-permute-done | bytes 131104 | tf_op jit(solution)/shard_map/ppermute | solution.py:24
  10.2 0.2 fusion.3
  10.4 0.0 copy-done.1
  10.4 0.2 fusion.6
  10.6 0.4 fusion.8
  11.1 0.3 convolution_convert_fusion
  11.4 1.6 %collective-permute-start.2 = (bf16[64,512]{1,0:T(8,128)(2,1)S(1)}, bf16[64,512]{1,0:T(8,128)(2,1)S(1)}, u32[]{:S(2)}, u32[]{:S(2)}) collective-permute-start(bf16[64,512]{1,0:T(8,128)(2,1)S(1)} %convolution_convert_fusion), channel_id=1, source_target_pairs={{0,4},{4,8},{8,12},{12,16},{16,20},{20,24},{24,28},{28,0},{1,5},{5... | collective-permute-start | bytes 196616 | tf_op jit(solution)/shard_map/ppermute | solution.py:24
  13.0 0.1 copy.8
  13.1 1.3 %collective-permute-start.3 = (f32[64,512]{1,0:T(8,128)S(1)}, f32[64,512]{1,0:T(8,128)S(1)}, u32[]{:S(2)}, u32[]{:S(2)}) collective-permute-start(f32[64,512]{1,0:T(8,128)S(1)} %slice_bitcast_fusion.1), channel_id=1, source_target_pairs={{0,28},{4,0},{8,4},{12,8},{16,12},{20,16},{24,20},{28,24},{1,29},{... | collective-permute-start | bytes 393224 | tf_op jit(solution)/shard_map/ppermute | solution.py:24
  14.4 1.8 %collective-permute-done.2 = bf16[64,512]{1,0:T(8,128)(2,1)S(1)} collective-permute-done((bf16[64,512]{1,0:T(8,128)(2,1)S(1)}, bf16[64,512]{1,0:T(8,128)(2,1)S(1)}, u32[]{:S(2)}, u32[]{:S(2)}) %collective-permute-start.2) | collective-permute-done | bytes 65568 | tf_op jit(solution)/shard_map/ppermute | solution.py:24
  16.2 0.7 %collective-permute-done.3 = f32[64,512]{1,0:T(8,128)S(1)} collective-permute-done((f32[64,512]{1,0:T(8,128)S(1)}, f32[64,512]{1,0:T(8,128)S(1)}, u32[]{:S(2)}, u32[]{:S(2)}) %collective-permute-start.3) | collective-permute-done | bytes 131104 | tf_op jit(solution)/shard_map/ppermute | solution.py:24
  16.9 0.2 fusion.1
  17.2 1.0 %fusion.7 = bf16[1,512,512]{2,1,0:T(8,128)(2,1)} fusion(bf16[1,512,512]{2,1,0:T(8,128)(2,1)S(1)} %copy-done.1, f32[1,8,64,512]{3,2,1,0:T(8,128)S(1)} %fusion.1, bf16[1,512,512]{2,1,0:T(8,128)(2,1)S(1)} %fusion.6), kind=kLoop, calls=%fused_computation.14 | loop fusion | flops 1572864 | bytes 2621440 | tf_op jit(solution)/shard_map/convert_element_type | solution.py:261
  18.2 40.1 %shard_map.62 = f32[512,512]{1,0:T(8,128)} custom-call(s32[1,512]{1,0:T(1,128)} %bitcast.68, bf16[512,512]{1,0:T(8,128)(2,1)} %bitcast.63), custom_call_target="tpu_custom_call" | custom-call | tf_op jit(solution)/shard_map/pallas_call | solution.py:230
  58.3 2.3 %copy.11 = f32[512,512]{1,0:T(8,128)} copy(f32[512,512]{1,0:T(8,128)} %shard_map.62) | data formatting | bytes 2097152
  (5 shorter events, 0.0 us)
Async XLA Ops:
  0.6 1.0 %copy-start = (bf16[1,512,512]{2,1,0:T(8,128)(2,1)S(1)}, bf16[1,512,512]{2,1,0:T(8,128)(2,1)}, u32[]{:S(2)}) copy-start(bf16[1,512,512]{2,1,0:T(8,128)(2,1)} %param.13) | copy-start | bytes 1572868
  3.2 0.7 %copy-start.2 = (s32[1,64]{1,0:T(1,128)S(1)}, s32[1,64]{1,0:T(1,128)}, u32[]{:S(2)}) copy-start(s32[1,64]{1,0:T(1,128)} %param.14) | copy-start | bytes 772
  4.1 3.5 %copy-start.3 = (s32[4]{0:T(128)S(1)}, s32[4]{0:T(128)}, u32[]{:S(2)}) copy-start(s32[4]{0:T(128)} %param.15) | copy-start | bytes 52
  4.1 5.4 %collective-permute-start = (bf16[64,512]{1,0:T(8,128)(2,1)S(1)}, bf16[64,512]{1,0:T(8,128)(2,1)S(1)}, u32[]{:S(2)}, u32[]{:S(2)}) collective-permute-start(bf16[64,512]{1,0:T(8,128)(2,1)S(1)} %convolution_convert_fusion.1), channel_id=1, source_target_pairs={{0,4},{4,8},{8,12},{12,16},{16,20},{20,24},{24,28},{28,0},{1,5},{5... | collective-permute-start | bytes 196616 | tf_op jit(solution)/shard_map/ppermute | solution.py:24
  4.7 5.5 %collective-permute-start.1 = (f32[64,512]{1,0:T(8,128)S(1)}, f32[64,512]{1,0:T(8,128)S(1)}, u32[]{:S(2)}, u32[]{:S(2)}) collective-permute-start(f32[64,512]{1,0:T(8,128)S(1)} %slice_bitcast_fusion.3), channel_id=1, source_target_pairs={{0,28},{4,0},{8,4},{12,8},{16,12},{20,16},{24,20},{28,24},{1,29},{... | collective-permute-start | bytes 393224 | tf_op jit(solution)/shard_map/ppermute | solution.py:24
  8.4 2.0 %copy-start.1 = (bf16[1,512,512]{2,1,0:T(8,128)(2,1)S(1)}, bf16[1,512,512]{2,1,0:T(8,128)(2,1)}, u32[]{:S(2)}) copy-start(bf16[1,512,512]{2,1,0:T(8,128)(2,1)} %param.12) | copy-start | bytes 1572868
  11.4 4.8 %collective-permute-start.2 = (bf16[64,512]{1,0:T(8,128)(2,1)S(1)}, bf16[64,512]{1,0:T(8,128)(2,1)S(1)}, u32[]{:S(2)}, u32[]{:S(2)}) collective-permute-start(bf16[64,512]{1,0:T(8,128)(2,1)S(1)} %convolution_convert_fusion), channel_id=1, source_target_pairs={{0,4},{4,8},{8,12},{12,16},{16,20},{20,24},{24,28},{28,0},{1,5},{5... | collective-permute-start | bytes 196616 | tf_op jit(solution)/shard_map/ppermute | solution.py:24
  13.1 3.8 %collective-permute-start.3 = (f32[64,512]{1,0:T(8,128)S(1)}, f32[64,512]{1,0:T(8,128)S(1)}, u32[]{:S(2)}, u32[]{:S(2)}) collective-permute-start(f32[64,512]{1,0:T(8,128)S(1)} %slice_bitcast_fusion.1), channel_id=1, source_target_pairs={{0,28},{4,0},{8,4},{12,8},{16,12},{20,16},{24,20},{28,24},{1,29},{... | collective-permute-start | bytes 393224 | tf_op jit(solution)/shard_map/ppermute | solution.py:24

commit v2 on v1

v2 whole, which is shorter than its diff:
```python
import functools

import jax
import jax.numpy as jnp
from jax import lax
from jax.experimental import pallas as pl
from jax.experimental.pallas import tpu as pltpu
from jax.sharding import PartitionSpec as P

PANEL = 128
PANELS = 4
EARLY = 2
LAG = 3
SUBLANES = 16

center_value = 0.5
half_width = 2.0

MESH = pl.DeviceIdType.MESH


def chunk_slots(parts):
    sequence = [(k, p) for k in range(EARLY) for p in range(parts - 1)]
    sequence += [(k, parts - 1) for k in range(EARLY)]
    sequence += [(k, p) for k in range(EARLY, PANELS) for p in range(parts)]
    slot = {pair: i for i, pair in enumerate(sequence)}
    return [[slot[k, p] for p in range(parts)] for k in range(PANELS)]


def filter_kernel(
    n, nb, groups, columns_ref, row_ref, col_ref, a_ref, v_ref, f_ref, out_ref,
    wide, first, ordered, low_out, top_out, low_in, top_in, face_send, face_recv,
    own, going_up, going_down, turned, part, arrived, gathered,
    up_send, up_recv, down_send, down_recv, rs_send, rs_recv, ag_send, ag_recv,
):
    me = lax.axis_index("mesh")
    z = lax.axis_index("band")
    rows, cols = v_ref.shape
    face = col_ref.shape[0]
    chunk = 2 * face
    parts = rows // chunk
    slots = chunk_slots(parts)
    total = PANELS * parts
    early = EARLY * (parts - 1)
    inner = slice(face, rows - face)
    low, top = slice(0, face), slice(rows - face, rows)
    bf16, f32 = jnp.bfloat16, jnp.float32
    slice_rows = arrived.shape[2]
    per_group = PANELS // groups
    per_panel = n // per_group

    barrier = pltpu.get_barrier_semaphore()

    @pl.loop(1, n)
    def _(d):
        pl.semaphore_signal(
            barrier, inc=1, device_id={"mesh": lax.rem(me + d, n)}, device_id_type=MESH
        )

    @pl.when(z > 0)
    def _():
        pl.semaphore_signal(barrier, inc=1, device_id={"band": z - 1}, device_id_type=MESH)

    @pl.when(z < nb - 1)
    def _():
        pl.semaphore_signal(barrier, inc=1, device_id={"band": z + 1}, device_id_type=MESH)

    def product_of(left, right):
        return jnp.dot(left, right, preferred_element_type=f32)

    positions = lax.broadcasted_iota(jnp.int32, (face, face), 1)
    to_top = (col_ref[...] == positions).astype(f32).astype(bf16)
    positions = lax.broadcasted_iota(jnp.int32, (face, face), 0)
    to_low = (row_ref[...] == positions).astype(f32).astype(bf16)
    following, previous = lax.rem(me + 1, n), lax.rem(me + n - 1, n)

    def low_copy(t):
        return pltpu.make_async_remote_copy(
            src_ref=low_out.at[t], dst_ref=low_in.at[t],
            send_sem=face_send.at[t, 0], recv_sem=face_recv.at[t, 0],
            device_id={"mesh": previous}, device_id_type=MESH,
        )

    def top_copy(t):
        return pltpu.make_async_remote_copy(
            src_ref=top_out.at[t], dst_ref=top_in.at[t],
            send_sem=face_send.at[t, 1], recv_sem=face_recv.at[t, 1],
            device_id={"mesh": following}, device_id_type=MESH,
        )

    def send_faces(t):
        low_out[t] = wide[low].astype(bf16)
        top_out[t] = product_of(to_low, wide[top].astype(bf16)).astype(bf16)
        low_copy(t).start()
        top_copy(t).start()

    def take_faces(t):
        low_copy(t).wait_recv()
        top_copy(t).wait_recv()
        wide[top] = wide[top] + product_of(to_top, low_in[t])
        wide[low] = wide[low] + top_in[t].astype(f32)

    def first_step(where):
        start = v_ref[where].astype(f32)
        first[where] = ((wide[where] - center_value * start) / half_width).astype(bf16)

    def second_step(where):
        start = v_ref[where].astype(f32)
        value = 2.0 * (wide[where] - center_value * first[where].astype(f32)) / half_width
        f_ref[where] = (value - start).astype(bf16)

    wide[...] = product_of(a_ref[...], v_ref[...])
    pl.semaphore_wait(barrier, n - 1 + jnp.minimum(z, 1) + jnp.minimum(nb - 1 - z, 1))

    send_faces(0)
    first_step(inner)
    here = lax.broadcasted_iota(jnp.int32, (cols, PANELS * PANEL), 0) + z * cols
    picker = (here == columns_ref[...]).astype(f32).astype(bf16)
    middle = slice(chunk, rows - chunk)
    left, right = slice(0, chunk), slice(rows - chunk, rows)
    so_far = product_of(a_ref[:, middle], first[middle])
    take_faces(0)
    first_step(low)
    first_step(top)
    wide[...] = (
        so_far
        + product_of(a_ref[:, left], first[left])
        + product_of(a_ref[:, right], first[right])
    )
    send_faces(1)
    second_step(inner)

    def own_chunks(which, values):
        picked = product_of(values, picker).astype(bf16)
        for k in range(PANELS):
            for i, p in enumerate(which):
                piece = picked[i * chunk:(i + 1) * chunk, k * PANEL:(k + 1) * PANEL]
                own[slots[k][p]] = piece

        @pl.when(z == 0)
        def _():
            for k in range(PANELS):
                for p in which:
                    going_up[slots[k][p]] = own[slots[k][p]]

        @pl.when(z == nb - 1)
        def _():
            for k in range(PANELS):
                for p in which:
                    going_down[slots[k][p]] = own[slots[k][p]]

    ordered[0:rows - chunk] = f_ref[inner]
    own_chunks(list(range(parts - 1)), ordered[0:rows - chunk])

    def sweep_copy(buffer, idx, send, recv, target):
        return pltpu.make_async_remote_copy(
            src_ref=buffer.at[idx], dst_ref=buffer.at[idx],
            send_sem=send.at[idx], recv_sem=recv.at[idx],
            device_id={"band": target}, device_id_type=MESH,
        )

    def pass_on(idx, buffer, send, recv, first, last, target):
        @pl.when(jnp.logical_and(idx >= 0, idx < total))
        def _():
            @pl.when(jnp.logical_not(first))
            def _():
                sweep_copy(buffer, idx, send, recv, target).wait_recv()
                buffer[idx] = own[idx] + buffer[idx]

            @pl.when(jnp.logical_not(last))
            def _():
                sweep_copy(buffer, idx, send, recv, target).start()

    above = lax.rem(z + 1, nb)
    below = lax.rem(z + nb - 1, nb)

    def step(s):
        pass_on(s - LAG * z, going_up, up_send, up_recv, z == 0, z == nb - 1, above)
        pass_on(
            s - LAG * (nb - 1 - z), going_down, down_send, down_recv, z == nb - 1, z == 0, below
        )

    def scatter_copy(g, d):
        target = lax.rem(me + d, n)
        return pltpu.make_async_remote_copy(
            src_ref=part.at[g, target], dst_ref=arrived.at[g, d],
            send_sem=rs_send.at[g, d], recv_sem=rs_recv.at[g, d],
            device_id={"mesh": target}, device_id_type=MESH,
        )

    def gather_copy(g, d, block):
        return pltpu.make_async_remote_copy(
            src_ref=gathered.at[g, block], dst_ref=gathered.at[g, block],
            send_sem=ag_send.at[g, d], recv_sem=ag_recv.at[g, d],
            device_id={"mesh": lax.rem(me + d, n)}, device_id_type=MESH,
        )

    def scatter(g):
        @pl.loop(1, n)
        def _(d):
            scatter_copy(g, d).start()

    def reduce(g):
        @pl.loop(1, n)
        def _(d):
            scatter_copy(g, d).wait_recv()
        summed = part[g, me].astype(jnp.float32)
        if n <= SUBLANES:
            for d in range(1, n):
                summed += arrived[g, d].astype(jnp.float32)
        else:
            summed = lax.fori_loop(
                1, n, lambda d, value: value + arrived[g, d].astype(jnp.float32), summed
            )
        gathered[g, me] = (summed).astype(jnp.bfloat16)

        @pl.loop(1, n)
        def _(d):
            gather_copy(g, d, me).start()

    def finish(g):
        @pl.loop(1, n)
        def _(d):
            gather_copy(g, d, lax.rem(me + n - d, n)).wait_recv()
        for p in range(per_group):
            k = g * per_group + p
            block = gathered[g, p * per_panel:(p + 1) * per_panel]
            out_ref[:, k * PANEL:(k + 1) * PANEL] = block.reshape(cols, PANEL)

    done = early

    @pl.loop(0, early)
    def _(s):
        step(s)

    take_faces(1)
    second_step(low)
    second_step(top)
    ordered[rows - chunk:rows - face] = f_ref[low]
    ordered[rows - face:rows] = f_ref[top]
    own_chunks([parts - 1], ordered[rows - chunk:rows])
    turned[...] = ordered[...].T
    for k in range(PANELS):
        until = max(done, LAG * (nb - 1) + slots[k][-1] + 1)

        @pl.loop(done, until)
        def _(s):
            step(s)
        done = until
        panel = jnp.concatenate(
            [going_up[i] + (going_down[i] - own[i]) for i in slots[k]], 0
        )
        product = jnp.dot(turned[...], panel, preferred_element_type=jnp.float32)
        g, p = k // per_group, k % per_group
        part[g, p * per_panel:(p + 1) * per_panel] = product.astype(jnp.bfloat16).reshape(
            per_panel, slice_rows, PANEL
        )
        if p == per_group - 1:
            scatter(g)
            if g > 0:
                reduce(g - 1)
            if g > 1:
                finish(g - 2)
    reduce(groups - 1)
    if groups > 1:
        finish(groups - 2)
    finish(groups - 1)

    @pl.loop(0, total)
    def _(idx):
        @pl.when(z < nb - 1)
        def _():
            sweep_copy(going_up, idx, up_send, up_recv, above).wait_send()

        @pl.when(z > 0)
        def _():
            sweep_copy(going_down, idx, down_send, down_recv, below).wait_send()

    for t in range(2):
        low_copy(t).wait_send()
        top_copy(t).wait_send()
    for g in range(groups):
        @pl.loop(1, n)
        def _(d):
            scatter_copy(g, d).wait_send()
            gather_copy(g, d, me).wait_send()


def on_device(n, nb, orbitals, element_matrix, face_map, panel_order):
    elements, rows, cols = orbitals.shape
    face = face_map.shape[1]
    groups = max(1, min(PANELS, PANELS * cols // (n * SUBLANES)))
    slice_rows = PANELS * cols // (groups * n)
    chunk = 2 * face
    total = PANELS * rows // chunk
    scale = float(rows * n) ** (-0.5)
    bf16 = jnp.bfloat16
    sweep = pltpu.VMEM((total, chunk, PANEL), bf16)
    blocks = pltpu.VMEM((groups, n, slice_rows, PANEL), bf16)
    faces = pltpu.VMEM((2, face, cols), bf16)
    square = pltpu.VMEM((rows, cols), bf16)
    dma = pltpu.SemaphoreType.DMA
    columns = (
        panel_order[:, None] * PANEL + jnp.arange(PANEL, dtype=jnp.int32)[None, :]
    ).reshape(1, PANELS * PANEL)
    filtered, margin = pl.pallas_call(
        functools.partial(filter_kernel, n, nb, groups),
        out_shape=(
            jax.ShapeDtypeStruct((rows, cols), bf16),
            jax.ShapeDtypeStruct((cols, PANELS * PANEL), bf16),
        ),
        in_specs=[pl.BlockSpec(memory_space=pltpu.VMEM)] * 5,
        out_specs=(pl.BlockSpec(memory_space=pltpu.VMEM),) * 2,
        scratch_shapes=[
            pltpu.VMEM((rows, cols), jnp.float32), square, square,
            faces, faces, faces, faces, dma((2, 2)), dma((2, 2)),
            sweep, sweep, sweep, pltpu.VMEM((cols, rows), bf16), blocks, blocks, blocks,
            dma((total,)), dma((total,)), dma((total,)), dma((total,)),
            dma((groups, n)), dma((groups, n)), dma((groups, n)), dma((groups, n)),
        ],
        compiler_params=pltpu.CompilerParams(collective_id=0, has_side_effects=True),
    )(
        columns, face_map, face_map.reshape(face, 1),
        element_matrix.reshape(rows, rows), orbitals.reshape(rows, cols),
    )
    return (filtered.reshape(elements, rows, cols), margin.astype(jnp.float32) * scale)


def solution(mesh):
    in_specs = (P("mesh", None, "band"), P("mesh", None, None), P("mesh", None), P())
    out_specs = (P("mesh", None, "band"), P("band", None))
    return jax.shard_map(
        functools.partial(on_device, mesh.shape["mesh"], mesh.shape["band"]),
        mesh=mesh, in_specs=in_specs, out_specs=out_specs, check_vma=False,
    )
```

time: 60.9 us -> 53 us (0.87)
  Pallas kernels: 40.1 us -> 46.5 us
  starting transfers between devices: 6.38 us -> 0 us
  waiting for transfers between devices: 4.23 us -> 0 us
  matrix products: 3.04 us -> 0 us
  local copies, waits for them, and re-layouts: 4.19 us -> 2.81 us
  other arithmetic: 1.89 us -> 2.87 us
    pallas_call x1, Pallas kernels: 40.1 us -> 46.5 us  [on_device(): pl.pallas_call(functools.partial(filter_kernel, n, nb, groups), out_shape...]
    ppermute x4 -> x0, starting transfers between devices: 6.38 us -> none  [passed_along(): lax.ppermute(shard, axis, [(i, (i + by) % devices) for i in range(devices)])]
    ppermute x4 -> x0, waiting for transfers between devices: 4.23 us -> none  [passed_along(): lax.ppermute(shard, axis, [(i, (i + by) % devices) for i in range(devices)])]
    dot_general x6 -> x0, matrix products: 3.04 us -> none  [the longest x2 1.91 us: operate(): jnp.einsum('enm,emo->eno', matrices, values, preferred_element_type=jnp.f...]
    mul x1 -> x2, other arithmetic: 0.01 us -> 2.22 us  [the longest x1 2.21 us: on_device(): margin.astype(jnp.float32) * scale]
    unnamed x11 -> x7, local copies, waits for them, and re-layouts: 4.17 us -> 2.1 us
    convert_element_type x2 -> x0, other arithmetic: 1.21 us -> none  [the longest x1 1.02 us: on_device(): filtered = second.astype(jnp.bfloat16)]
    reshape x0 -> x1, local copies, waits for them, and re-layouts: none -> 0.71 us  [on_device(): face_map.reshape(face, 1)]
  transfers between devices with their start and end apart: 4 -> 0, of which waited for: 4 -> 0; matrix products, arithmetic and copies ran while one was open for 1% -> 0% of each run, Pallas kernels for 0% -> 0%
where the time goes in v2:
time: 53 us; the launch traced here: 52.8 us
  Pallas kernels  46.5 us (88%)
  other arithmetic  2.87 us (5%)
  local copies, waits for them, and re-layouts  2.81 us (5%)
  between operations  0.66 us (1%)
    pallas_call x1, Pallas kernels, on_device(): pl.pallas_call(functools.partial(filter_kernel, n, nb, groups), out_shape...  46.5 us
    mul x1, other arithmetic, on_device(): margin.astype(jnp.float32) * scale  2.21 us
    unnamed x7, local copies, waits for them, and re-layouts  2.1 us

profile of v2, /device:TPU:0, one launch (start us, length us, event | category | flops | bytes accessed | tf_op | source)
XLA Modules:
  0.0 52.8 jit_solution(3059116059054461018)
XLA Ops:
  0.6 0.0 copy-start.2
  0.6 0.6 %copy-done.2 = s32[4]{0:T(128)S(1)} copy-done((s32[4]{0:T(128)S(1)}, s32[4]{0:T(128)}, u32[]{:S(2)}) %copy-start.2) | copy-done | bytes 40
  1.3 0.7 %iota_add_fusion = s32[4,128]{1,0:T(4,128)} fusion(s32[4]{0:T(128)S(1)} %broadcast_multiply_fusion), kind=kLoop, calls=%fused_computation.1 | loop fusion | flops 512 | bytes 2064 | tf_op jit(solution)/shard_map/add | solution.py:304
  1.9 0.0 copy-start.1
  1.9 0.7 %copy-done.1 = s32[1,64]{1,0:T(1,128)S(1)} copy-done((s32[1,64]{1,0:T(1,128)S(1)}, s32[1,64]{1,0:T(1,128)}, u32[]{:S(2)}) %copy-start.1) | copy-done | bytes 280
  2.6 0.7 %copy.6.col_ref = s32[64,1]{1,0:T(8,128)} copy(s32[64,1]{0,1:T(1,128)S(1)} %bitcast.9) | data formatting | bytes 512 | tf_op jit(solution)/shard_map/reshape | solution.py:323
  3.3 46.5 %shard_map.59 = (bf16[512,512]{1,0:T(8,128)(2,1)}, bf16[512,512]{1,0:T(8,128)(2,1)}) custom-call(s32[1,512]{1,0:T(1,128)} %bitcast.8, s32[1,64]{1,0:T(1,128)} %row_ref.1, s32[64,1]{1,0:T(8,128)} %copy.6.col_ref, bf16[512,512]{1,0:T(8,128)(2,1)} %bitcast.6, bf16[512,512]{1,0:T(8,128)(2,1)} %bitcast.7), custom_call_target="tpu_custom_call" | custom-call | tf_op jit(solution)/shard_map/pallas_call | solution.py:306
  49.8 0.0 copy-start
  49.8 2.2 %convert_multiply_fusion = f32[512,512]{1,0:T(8,128)} fusion(bf16[512,512]{1,0:T(8,128)(2,1)} %get-tuple-element.5), kind=kLoop, calls=%fused_computation | loop fusion | flops 524288 | bytes 1572864 | tf_op jit(solution)/shard_map/mul | solution.py:326
  52.0 0.0 copy-done
  52.0 0.8 %copy.8 = bf16[1,512,512]{2,1,0:T(8,128)(2,1)} copy(bf16[1,512,512]{2,1,0:T(8,128)(2,1)S(1)} %bitcast.5) | data formatting | bytes 1048576
  (1 shorter events, 0.0 us)
Async XLA Ops:
  0.6 0.7 %copy-start.2 = (s32[4]{0:T(128)S(1)}, s32[4]{0:T(128)}, u32[]{:S(2)}) copy-start(s32[4]{0:T(128)} %param.7) | copy-start | bytes 52
  1.9 0.7 %copy-start.1 = (s32[1,64]{1,0:T(1,128)S(1)}, s32[1,64]{1,0:T(1,128)}, u32[]{:S(2)}) copy-start(s32[1,64]{1,0:T(1,128)} %row_ref.1) | copy-start | bytes 772
  49.8 2.2 %copy-start = (bf16[512,512]{1,0:T(8,128)(2,1)S(1)}, bf16[512,512]{1,0:T(8,128)(2,1)}, u32[]{:S(2)}) copy-start(bf16[512,512]{1,0:T(8,128)(2,1)} %get-tuple-element.4) | copy-start | bytes 1572868

commit v3 on v2

--- a/solution.py
+++ b/solution.py
@@ -10,7 +10,7 @@
 PANEL = 128
 PANELS = 4
 EARLY = 2
-LAG = 3
+LAG = 5
 SUBLANES = 16
 
 center_value = 0.5
@@ -28,7 +28,7 @@
 
 
 def filter_kernel(
-    n, nb, groups, columns_ref, row_ref, col_ref, a_ref, v_ref, f_ref, out_ref,
+    n, nb, groups, order_ref, row_ref, a_ref, v_ref, f_ref, out_ref,
     wide, first, ordered, low_out, top_out, low_in, top_in, face_send, face_recv,
     own, going_up, going_down, turned, part, arrived, gathered,
     up_send, up_recv, down_send, down_recv, rs_send, rs_recv, ag_send, ag_recv,
@@ -36,7 +36,7 @@
     me = lax.axis_index("mesh")
     z = lax.axis_index("band")
     rows, cols = v_ref.shape
-    face = col_ref.shape[0]
+    face = row_ref.shape[1]
     chunk = 2 * face
     parts = rows // chunk
     slots = chunk_slots(parts)
@@ -68,10 +68,9 @@
     def product_of(left, right):
         return jnp.dot(left, right, preferred_element_type=f32)
 
-    positions = lax.broadcasted_iota(jnp.int32, (face, face), 1)
-    to_top = (col_ref[...] == positions).astype(f32).astype(bf16)
     positions = lax.broadcasted_iota(jnp.int32, (face, face), 0)
-    to_low = (row_ref[...] == positions).astype(f32).astype(bf16)
+    one_hot = (row_ref[...] == positions).astype(f32)
+    to_low, to_top = one_hot.astype(bf16), one_hot.T.astype(bf16)
     following, previous = lax.rem(me + 1, n), lax.rem(me + n - 1, n)
 
     def low_copy(t):
@@ -109,25 +108,32 @@
         value = 2.0 * (wide[where] - center_value * first[where].astype(f32)) / half_width
         f_ref[where] = (value - start).astype(bf16)
 
-    wide[...] = product_of(a_ref[...], v_ref[...])
+    both = product_of(jnp.concatenate([a_ref[low], a_ref[top]], 0), v_ref[...])
+    wide[low], wide[top] = both[:face], both[face:]
     pl.semaphore_wait(barrier, n - 1 + jnp.minimum(z, 1) + jnp.minimum(nb - 1 - z, 1))
 
     send_faces(0)
+    wide[inner] = product_of(a_ref[inner], v_ref[...])
     first_step(inner)
-    here = lax.broadcasted_iota(jnp.int32, (cols, PANELS * PANEL), 0) + z * cols
-    picker = (here == columns_ref[...]).astype(f32).astype(bf16)
+    here = lax.broadcasted_iota(jnp.int32, (cols, PANEL), 0) + z * cols
+    here = here - lax.broadcasted_iota(jnp.int32, (cols, PANEL), 1)
+    picker = jnp.concatenate(
+        [(here == order_ref[k] * PANEL).astype(f32).astype(bf16) for k in range(PANELS)], 1
+    )
     middle = slice(chunk, rows - chunk)
     left, right = slice(0, chunk), slice(rows - chunk, rows)
     so_far = product_of(a_ref[:, middle], first[middle])
     take_faces(0)
     first_step(low)
     first_step(top)
-    wide[...] = (
-        so_far
-        + product_of(a_ref[:, left], first[left])
-        + product_of(a_ref[:, right], first[right])
+    outer_left = jnp.concatenate([a_ref[:, left], a_ref[:, right]], 1)
+    outer_right = jnp.concatenate([first[left], first[right]], 0)
+    both = product_of(
+        jnp.concatenate([outer_left[low], outer_left[top]], 0), outer_right
     )
+    wide[low], wide[top] = so_far[low] + both[:face], so_far[top] + both[face:]
     send_faces(1)
+    wide[inner] = so_far[inner] + product_of(outer_left[inner], outer_right)
     second_step(inner)
 
     def own_chunks(which, values):
@@ -257,14 +263,12 @@
         )
         if p == per_group - 1:
             scatter(g)
-            if g > 0:
-                reduce(g - 1)
             if g > 1:
-                finish(g - 2)
-    reduce(groups - 1)
-    if groups > 1:
-        finish(groups - 2)
-    finish(groups - 1)
+                reduce(g - 2)
+    for g in range(max(groups - 2, 0), groups):
+        reduce(g)
+    for g in range(groups):
+        finish(g)
 
     @pl.loop(0, total)
     def _(idx):
@@ -284,6 +288,11 @@
         def _(d):
             scatter_copy(g, d).wait_send()
             gather_copy(g, d, me).wait_send()
+
+
+def write_kernel(scale, f_ref, m_ref, filtered_ref, margin_ref):
+    filtered_ref[...] = f_ref[...]
+    margin_ref[...] = m_ref[...].astype(jnp.float32) * scale
 
 
 def on_device(n, nb, orbitals, element_matrix, face_map, panel_order):
@@ -300,16 +309,14 @@
     faces = pltpu.VMEM((2, face, cols), bf16)
     square = pltpu.VMEM((rows, cols), bf16)
     dma = pltpu.SemaphoreType.DMA
-    columns = (
-        panel_order[:, None] * PANEL + jnp.arange(PANEL, dtype=jnp.int32)[None, :]
-    ).reshape(1, PANELS * PANEL)
     filtered, margin = pl.pallas_call(
         functools.partial(filter_kernel, n, nb, groups),
         out_shape=(
             jax.ShapeDtypeStruct((rows, cols), bf16),
             jax.ShapeDtypeStruct((cols, PANELS * PANEL), bf16),
         ),
-        in_specs=[pl.BlockSpec(memory_space=pltpu.VMEM)] * 5,
+        in_specs=[pl.BlockSpec(memory_space=pltpu.SMEM)]
+        + [pl.BlockSpec(memory_space=pltpu.VMEM)] * 3,
         out_specs=(pl.BlockSpec(memory_space=pltpu.VMEM),) * 2,
         scratch_shapes=[
             pltpu.VMEM((rows, cols), jnp.float32), square, square,
@@ -320,10 +327,23 @@
         ],
         compiler_params=pltpu.CompilerParams(collective_id=0, has_side_effects=True),
     )(
-        columns, face_map, face_map.reshape(face, 1),
+        panel_order, face_map,
         element_matrix.reshape(rows, rows), orbitals.reshape(rows, cols),
     )
-    return (filtered.reshape(elements, rows, cols), margin.astype(jnp.float32) * scale)
+    steps = 1
+    narrow = pl.BlockSpec((rows // steps, cols), lambda i: (i, 0))
+    wide = pl.BlockSpec((cols // steps, PANELS * PANEL), lambda i: (i, 0))
+    filtered, margin = pl.pallas_call(
+        functools.partial(write_kernel, scale),
+        grid=(steps,),
+        out_shape=(
+            jax.ShapeDtypeStruct((rows, cols), bf16),
+            jax.ShapeDtypeStruct((cols, PANELS * PANEL), jnp.float32),
+        ),
+        in_specs=[narrow, wide],
+        out_specs=(narrow, wide),
+    )(filtered, margin)
+    return (filtered.reshape(elements, rows, cols), margin)
 
 
 def solution(mesh):

time: 53 us -> 44.5 us (0.84)
  Pallas kernels: 46.5 us -> 43.6 us
  other arithmetic: 2.87 us -> 0 us
  local copies, waits for them, and re-layouts: 2.81 us -> 0 us
    pallas_call x1, Pallas kernels: 46.5 us -> 41.3 us  [on_device(): pl.pallas_call(functools.partial(filter_kernel, n, nb, groups), out_shape...]
    pallas_call x0 -> x1, Pallas kernels: none -> 2.38 us  [on_device(): pl.pallas_call(functools.partial(write_kernel, scale), grid=(steps,), out...]
    mul x2 -> x0, other arithmetic: 2.22 us -> none  [the longest x1 2.21 us: on_device(): margin.astype(jnp.float32) * scale]
    unnamed x7 -> x0, local copies, waits for them, and re-layouts: 2.1 us -> none
    reshape x1 -> x0, local copies, waits for them, and re-layouts: 0.71 us -> none  [on_device(): face_map.reshape(face, 1)]
    add x1 -> x0, other arithmetic: 0.65 us -> none  [on_device(): panel_order[:, None] * PANEL + jnp.arange(PANEL, dtype=jnp.int32)[None, :]]
where the time goes in v3:
time: 44.5 us; the launch traced here: 44.3 us
  Pallas kernels  43.6 us (98%)
  between operations  0.64 us (1%)
    pallas_call x1, Pallas kernels, on_device(): pl.pallas_call(functools.partial(filter_kernel, n, nb, groups), out_shape...  41.3 us
    pallas_call x1, Pallas kernels, on_device(): pl.pallas_call(functools.partial(write_kernel, scale), grid=(steps,), out...  2.38 us

profile of v3, /device:TPU:0, one launch (start us, length us, event | category | flops | bytes accessed | tf_op | source)
XLA Modules:
  0.0 44.3 jit_solution(12710686474211024809)
XLA Ops:
  0.6 41.3 %shard_map.59 = (bf16[512,512]{1,0:T(8,128)(2,1)}, bf16[512,512]{1,0:T(8,128)(2,1)}) custom-call(s32[4]{0:T(128)} %order_ref.1, s32[1,64]{1,0:T(1,128)} %row_ref.1, bf16[512,512]{1,0:T(8,128)(2,1)} %bitcast.3, bf16[512,512]{1,0:T(8,128)(2,1)} %bitcast.4), custom_call_target="tpu_custom_call" | custom-call | tf_op jit(solution)/shard_map/pallas_call | solution.py:312
  41.9 2.4 %shard_map.60 = (bf16[512,512]{1,0:T(8,128)(2,1)}, f32[512,512]{1,0:T(8,128)}) custom-call(bf16[512,512]{1,0:T(8,128)(2,1)} %get-tuple-element.6.f_ref, bf16[512,512]{1,0:T(8,128)(2,1)} %get-tuple-element.7.m_ref), custom_call_target="tpu_custom_call" | custom-call | tf_op jit(solution)/shard_map/pallas_call | solution.py:336

commit v4 on v3

--- a/solution.py
+++ b/solution.py
@@ -28,8 +28,8 @@
 
 
 def filter_kernel(
-    n, nb, groups, order_ref, row_ref, a_ref, v_ref, f_ref, out_ref,
-    wide, first, ordered, low_out, top_out, low_in, top_in, face_send, face_recv,
+    n, nb, groups, order_ref, row_ref, a_hbm, v_hbm, f_hbm, out_ref,
+    a_ref, v_ref, f_ref, local, wide, first, ordered, low_out, top_out, low_in, top_in, face_send, face_recv,
     own, going_up, going_down, turned, part, arrived, gathered,
     up_send, up_recv, down_send, down_recv, rs_send, rs_recv, ag_send, ag_recv,
 ):
@@ -49,6 +49,11 @@
     per_group = PANELS // groups
     per_panel = n // per_group
 
+    load_a = pltpu.make_async_copy(a_hbm, a_ref, local.at[0])
+    load_v = pltpu.make_async_copy(v_hbm, v_ref, local.at[1])
+    store_f = pltpu.make_async_copy(f_ref, f_hbm, local.at[2])
+    load_a.start()
+    load_v.start()
     barrier = pltpu.get_barrier_semaphore()
 
     @pl.loop(1, n)
@@ -108,18 +113,20 @@
         value = 2.0 * (wide[where] - center_value * first[where].astype(f32)) / half_width
         f_ref[where] = (value - start).astype(bf16)
 
-    both = product_of(jnp.concatenate([a_ref[low], a_ref[top]], 0), v_ref[...])
-    wide[low], wide[top] = both[:face], both[face:]
-    pl.semaphore_wait(barrier, n - 1 + jnp.minimum(z, 1) + jnp.minimum(nb - 1 - z, 1))
-
-    send_faces(0)
-    wide[inner] = product_of(a_ref[inner], v_ref[...])
-    first_step(inner)
     here = lax.broadcasted_iota(jnp.int32, (cols, PANEL), 0) + z * cols
     here = here - lax.broadcasted_iota(jnp.int32, (cols, PANEL), 1)
     picker = jnp.concatenate(
         [(here == order_ref[k] * PANEL).astype(f32).astype(bf16) for k in range(PANELS)], 1
     )
+    load_a.wait()
+    load_v.wait()
+    both = product_of(jnp.concatenate([a_ref[low], a_ref[top]], 0), v_ref[...])
+    wide[low], wide[top] = both[:face], both[face:]
+    pl.semaphore_wait(barrier, n - 1 + jnp.minimum(z, 1) + jnp.minimum(nb - 1 - z, 1))
+
+    send_faces(0)
+    wide[inner] = product_of(a_ref[inner], v_ref[...])
+    first_step(inner)
     middle = slice(chunk, rows - chunk)
     left, right = slice(0, chunk), slice(rows - chunk, rows)
     so_far = product_of(a_ref[:, middle], first[middle])
@@ -242,6 +249,7 @@
     take_faces(1)
     second_step(low)
     second_step(top)
+    store_f.start()
     ordered[rows - chunk:rows - face] = f_ref[low]
     ordered[rows - face:rows] = f_ref[top]
     own_chunks([parts - 1], ordered[rows - chunk:rows])
@@ -280,6 +288,7 @@
         def _():
             sweep_copy(going_down, idx, down_send, down_recv, below).wait_send()
 
+    store_f.wait()
     for t in range(2):
         low_copy(t).wait_send()
         top_copy(t).wait_send()
@@ -316,9 +325,13 @@
             jax.ShapeDtypeStruct((cols, PANELS * PANEL), bf16),
         ),
         in_specs=[pl.BlockSpec(memory_space=pltpu.SMEM)]
-        + [pl.BlockSpec(memory_space=pltpu.VMEM)] * 3,
-        out_specs=(pl.BlockSpec(memory_space=pltpu.VMEM),) * 2,
+        + [pl.BlockSpec(memory_space=pltpu.VMEM)]
+        + [pl.BlockSpec(memory_space=pl.ANY)] * 2,
+        out_specs=(
+            pl.BlockSpec(memory_space=pl.ANY), pl.BlockSpec(memory_space=pltpu.VMEM)
+        ),
         scratch_shapes=[
+            pltpu.VMEM((rows, rows), bf16), square, square, dma((3,)),
             pltpu.VMEM((rows, cols), jnp.float32), square, square,
             faces, faces, faces, faces, dma((2, 2)), dma((2, 2)),
             sweep, sweep, sweep, pltpu.VMEM((cols, rows), bf16), blocks, blocks, blocks,

time: 44.5 us -> 44 us (0.989)
    pallas_call x1, Pallas kernels: 41.3 us -> 40.8 us  [on_device(): pl.pallas_call(functools.partial(filter_kernel, n, nb, groups), out_shape...]
where the time goes in v4:
time: 44 us; the launch traced here: 43.8 us
  Pallas kernels  43.2 us (98%)
  between operations  0.64 us (1%)
    pallas_call x1, Pallas kernels, on_device(): pl.pallas_call(functools.partial(filter_kernel, n, nb, groups), out_shape...  40.8 us
    pallas_call x1, Pallas kernels, on_device(): pl.pallas_call(functools.partial(write_kernel, scale), grid=(steps,), out...  2.38 us

profile of v4, /device:TPU:0, one launch (start us, length us, event | category | flops | bytes accessed | tf_op | source)
XLA Modules:
  0.0 43.8 jit_solution(13229972041547715535)
XLA Ops:
  0.6 40.8 %shard_map.59 = (bf16[512,512]{1,0:T(8,128)(2,1)}, bf16[512,512]{1,0:T(8,128)(2,1)}) custom-call(s32[4]{0:T(128)} %order_ref.1, s32[1,64]{1,0:T(1,128)} %row_ref.1, bf16[512,512]{1,0:T(8,128)(2,1)} %bitcast.3, bf16[512,512]{1,0:T(8,128)(2,1)} %bitcast.4), custom_call_target="tpu_custom_call" | custom-call | tf_op jit(solution)/shard_map/pallas_call | solution.py:321
  41.4 2.4 %shard_map.60 = (bf16[512,512]{1,0:T(8,128)(2,1)}, f32[512,512]{1,0:T(8,128)}) custom-call(bf16[512,512]{1,0:T(8,128)(2,1)} %get-tuple-element.6.f_ref, bf16[512,512]{1,0:T(8,128)(2,1)} %get-tuple-element.7.m_ref), custom_call_target="tpu_custom_call" | custom-call | tf_op jit(solution)/shard_map/pallas_call | solution.py:349
